TPU v7x, 32 devices: a whole 2x2x4 slice. The times are simulated.
32 devices in a mesh: row: 8 (over y, x, core), col: 4 (over z).
Axes of the slice: x: 2, y: 2, z: 4, core: 2. Of those that a mesh axis runs over, the one named last changes fastest.
Arguments:
- earlier_blocks: bfloat16 [32, 8, 128, 128], P('row', 'col'), may hold values from -0.5 to 0.5
- later_blocks: bfloat16 [8, 32, 128, 128], P('row', 'col'), may hold values from -6 to 6
- earlier_pattern: int32 [32, 8], P('row', 'col'), may hold values from 0 to 1, as said below
- later_pattern: int32 [8, 32], P('row', 'col'), may hold values from 0 to 1, as said below
- triples: int32 [32, 32, 48], P('row', 'col'), may hold values from 0 to 7
Outputs:
- composed: float32 [32, 32, 128, 128], P('row', 'col')
Inputs may be any that keep to these rules, and one draw needn't show every extreme that they name: `earlier_pattern`: in each aligned share of 4 x 2 entries held by one device, at most 4 entries are 1, and exactly 4 in some share. `later_pattern`: in each aligned share of 1 x 8 entries held by one device, at most 4 entries are 1, and exactly 4 in some share.
All inputs are finite; a program needn't handle non-finite values.
Results may differ from a plain program's by a relative error of at most 0.0003.
Values may be sent and summed in bfloat16 or wider, within the bound.
A program may use at most 256 MiB of HBM per device.

v0:
```python
import jax
import jax.numpy as jnp
from jax import lax
from jax.sharding import PartitionSpec as P


def compose_blocks(earlier_full, later_full, triples):
    count_rows = triples.shape[0]
    middle = earlier_full.shape[1]
    middle_numbers = jnp.arange(middle, dtype=jnp.int32)
    counts = jnp.sum(
        (triples[:, :, :, None] == middle_numbers[None, None, None, :]).astype(jnp.float32), axis=2
    )
    results = []
    for row_number in range(count_rows):
        products = jnp.einsum(
            "kab,kjbc->kjac",
            earlier_full[row_number],
            later_full,
            preferred_element_type=jnp.float32,
        )
        results.append(
            jnp.einsum(
                "jk,kjac->jac", counts[row_number], products, precision=lax.Precision.HIGHEST
            )
        )
    return jnp.stack(results, axis=0)


def on_device(earlier_blocks, later_blocks, earlier_pattern, later_pattern, triples):
    masked_early = earlier_blocks * earlier_pattern[:, :, None, None].astype(earlier_blocks.dtype)
    earlier_full = lax.all_gather(masked_early, "col", axis=1, tiled=True)
    masked_late = later_blocks * later_pattern[:, :, None, None].astype(later_blocks.dtype)
    later_full = lax.all_gather(masked_late, "row", axis=0, tiled=True)
    return compose_blocks(earlier_full, later_full, triples)


def solution(mesh):
    return jax.shard_map(
        on_device,
        mesh=mesh,
        in_specs=(
            P("row", "col", None, None),
            P("row", "col", None, None),
            P("row", "col"),
            P("row", "col"),
            P("row", "col", None),
        ),
        out_specs=P("row", "col", None, None),
        check_vma=False,
    )
```

profile of v0, /device:TPU:0, one launch (start us, length us, event | category | flops | bytes accessed | tf_op | source)
XLA Modules:
  0.0 129.0 jit_solution(241129378847575528)
XLA Ops:
  6.5 0.0 all-gather.5.cloned.1.call-start
  6.5 0.7 convert_element_type.21
  7.2 0.1 copy.8
  7.3 1.7 %broadcast_multiply_fusion = bf16[4,2,128,128]{3,2,1,0:T(8,128)(2,1)} fusion(bf16[4,2,128,128]{3,2,1,0:T(8,128)(2,1)} %param.5, bf16[4,2]{1,0:T(4,128)(2,1)S(1)} %copy.8), kind=kLoop, calls=%fused_computation.9 | loop fusion | flops 131072 | bytes 524304 | tf_op jit(solution)/shard_map/mul | solution.py:31
  9.1 0.0 all-gather.5.cloned.1.call-update
  9.1 0.0 all-gather.3.cloned.1.call-start
  9.1 0.7 convert_bitcast_fusion
  9.8 1.7 %broadcast_multiply_fusion.1 = bf16[1,8,128,128]{3,2,1,0:T(8,128)(2,1)} fusion(bf16[1,8,128,128]{3,2,1,0:T(8,128)(2,1)} %param.6, bf16[8]{0:T(256)(128)(2,1)S(1)} %convert_bitcast_fusion), kind=kLoop, calls=%fused_computation.10 | loop fusion | flops 131072 | bytes 524304 | tf_op jit(solution)/shard_map/mul | solution.py:33
  11.5 0.0 all-gather.3.cloned.1.call-update
  11.6 0.8 convert_reduce_fusion
  12.4 27.5 %all-gather.5.cloned.1.call-done = bf16[4,8,128,128]{3,2,1,0:T(8,128)(2,1)} async-done(((bf16[4,2,128,128]{3,2,1,0:T(8,128)(2,1)}), bf16[4,8,128,128]{3,2,1,0:T(8,128)(2,1)}) %all-gather.5.cloned.1.call-update) | async-done | bytes 1048592 | tf_op jit(solution)/shard_map/all_gather | solution.py:32
  40.0 29.1 %all-gather.3.cloned.1.call-done = bf16[8,8,128,128]{3,2,1,0:T(8,128)(2,1)} async-done(((bf16[1,8,128,128]{3,2,1,0:T(8,128)(2,1)}), bf16[8,8,128,128]{3,2,1,0:T(8,128)(2,1)}) %all-gather.3.cloned.1.call-update) | async-done | bytes 2097168 | tf_op jit(solution)/shard_map/all_gather | solution.py:34
  69.0 4.4 %convolution_bitcast_fusion = f32[8,8,128,128]{2,3,1,0:T(8,128)} fusion(bf16[8,8,128,128]{3,2,1,0:T(8,128)(2,1)} %all-gather.3.cloned.1.call-done, bf16[4,8,128,128]{3,2,1,0:T(8,128)(2,1)} %all-gather.5.cloned.1.call-done), kind=kOutput, calls=%fused_computation | convolution fusion | flops 268435456 | bytes 6553600 | tf_op jit(solution)/shard_map/kab,kjbc->kjac/dot_general | solution.py:16
  73.4 0.0 copy-start
  73.4 0.0 copy-start.4
  73.4 5.5 %copy.31 = f32[8,8,128,128]{3,0,2,1:T(8,128)} copy(f32[8,8,128,128]{2,3,1,0:T(8,128)} %convolution_bitcast_fusion) | data formatting | bytes 8388608 | tf_op jit(solution)/shard_map/kab,kjbc->kjac/transpose | solution.py:16
  78.9 0.0 copy-done
  78.9 0.0 copy-done.4
  78.9 2.8 %convolution_bitcast_fusion.1 = f32[8,8,128,128]{2,3,1,0:T(8,128)} fusion(bf16[8,8,128,128]{3,2,1,0:T(8,128)(2,1)S(1)} %copy-done, bf16[4,8,128,128]{3,2,1,0:T(8,128)(2,1)S(1)} %copy-done.4), kind=kOutput, calls=%fused_computation.1 | convolution fusion | flops 268435456 | bytes 6553600 | tf_op jit(solution)/shard_map/kab,kjbc->kjac/dot_general | solution.py:16
  81.7 5.4 %copy.26 = f32[8,8,128,128]{3,0,2,1:T(8,128)} copy(f32[8,8,128,128]{2,3,1,0:T(8,128)} %convolution_bitcast_fusion.1) | data formatting | bytes 8388608 | tf_op jit(solution)/shard_map/kab,kjbc->kjac/transpose | solution.py:16
  87.1 2.7 %convolution_bitcast_fusion.2 = f32[8,8,128,128]{2,3,1,0:T(8,128)} fusion(bf16[8,8,128,128]{3,2,1,0:T(8,128)(2,1)S(1)} %copy-done, bf16[4,8,128,128]{3,2,1,0:T(8,128)(2,1)S(1)} %copy-done.4), kind=kOutput, calls=%fused_computation.2 | convolution fusion | flops 268435456 | bytes 6553600 | tf_op jit(solution)/shard_map/kab,kjbc->kjac/dot_general | solution.py:16
  89.8 5.4 %copy.21 = f32[8,8,128,128]{3,0,2,1:T(8,128)} copy(f32[8,8,128,128]{2,3,1,0:T(8,128)} %convolution_bitcast_fusion.2) | data formatting | bytes 8388608 | tf_op jit(solution)/shard_map/kab,kjbc->kjac/transpose | solution.py:16
  95.2 2.7 %convolution_bitcast_fusion.3 = f32[8,8,128,128]{2,3,1,0:T(8,128)} fusion(bf16[8,8,128,128]{3,2,1,0:T(8,128)(2,1)S(1)} %copy-done, bf16[4,8,128,128]{3,2,1,0:T(8,128)(2,1)S(1)} %copy-done.4), kind=kOutput, calls=%fused_computation.3 | convolution fusion | flops 268435456 | bytes 6553600 | tf_op jit(solution)/shard_map/kab,kjbc->kjac/dot_general | solution.py:16
  98.0 5.3 %copy.16 = f32[8,8,128,128]{3,0,2,1:T(8,128)} copy(f32[8,8,128,128]{2,3,1,0:T(8,128)} %convolution_bitcast_fusion.3) | data formatting | bytes 8388608 | tf_op jit(solution)/shard_map/kab,kjbc->kjac/transpose | solution.py:16
  103.3 0.0 copy-start.1
  103.3 0.0 copy-start.2
  103.3 6.1 %fusion.4 = f32[8,1,128,128]{3,1,2,0:T(1,128)S(1)} fusion(f32[8,8,1,1]{1,2,3,0:T(1,128)S(1)} %bitcast.85, f32[8,8,128,128]{3,0,2,1:T(8,128)} %copy.31), kind=kOutput, calls=%fused_computation.18 | convolution fusion | flops 12582912 | bytes 4718848 | tf_op jit(solution)/shard_map/jk,kjac->jac/dot_general | solution.py:23
  109.4 0.0 copy-done.1
  109.4 0.0 copy-start.3
  109.5 3.7 %fusion.3 = f32[8,1,128,128]{3,1,2,0:T(1,128)S(1)} fusion(f32[8,8,1,1]{1,2,3,0:T(1,128)S(1)} %bitcast.84, f32[8,8,128,128]{3,0,2,1:T(8,128)S(1)} %copy-done.1), kind=kOutput, calls=%fused_computation.17 | convolution fusion | flops 12582912 | bytes 4718848 | tf_op jit(solution)/shard_map/jk,kjac->jac/dot_general | solution.py:23
  113.2 0.0 copy-done.2
  113.2 3.7 %fusion.2 = f32[8,1,128,128]{3,1,2,0:T(1,128)S(1)} fusion(f32[8,8,1,1]{1,2,3,0:T(1,128)S(1)} %bitcast.83, f32[8,8,128,128]{3,0,2,1:T(8,128)S(1)} %copy-done.2), kind=kOutput, calls=%fused_computation.16 | convolution fusion | flops 12582912 | bytes 4718848 | tf_op jit(solution)/shard_map/jk,kjac->jac/dot_general | solution.py:23
  116.9 0.0 copy-done.3
  117.0 3.7 %fusion.1 = f32[8,1,128,128]{3,1,2,0:T(1,128)S(1)} fusion(f32[8,8,1,1]{1,2,3,0:T(1,128)S(1)} %bitcast.82, f32[8,8,128,128]{3,0,2,1:T(8,128)S(1)} %copy-done.3), kind=kOutput, calls=%fused_computation.15 | convolution fusion | flops 12582912 | bytes 4718848 | tf_op jit(solution)/shard_map/jk,kjac->jac/dot_general | solution.py:23
  120.7 1.5 %pad_maximum_fusion = f32[4,8,128,128]{3,2,1,0:T(8,128)} fusion(f32[1,8,128,128]{3,2,1,0:T(8,128)S(1)} %bitcast.78, f32[1,8,128,128]{3,2,1,0:T(8,128)S(1)} %bitcast.79, f32[1,8,128,128]{3,2,1,0:T(8,128)S(1)} %bitcast.80, f32[1,8,128,128]{3,2,1,0:T(8,128)S(1)} %bitcast.81), kind=kLoop, calls=%fused_computation.4 | loop fusion | flops 1572864 | bytes 4194304 | tf_op jit(solution)/shard_map/stack | solution.py:27
  (1 shorter events, 0.0 us)
Async XLA Ops:
  6.5 33.4 %all-gather.5.cloned.1.call-start = ((), (), s32[]{:S(2)}) async-start(), calls=%async_computation.1 | async-start | bytes 1310720 | tf_op jit(solution)/shard_map/all_gather | solution.py:32
  9.1 59.9 %all-gather.3.cloned.1.call-start = ((), (), s32[]{:S(2)}) async-start(), calls=%async_computation | async-start | bytes 2359296 | tf_op jit(solution)/shard_map/all_gather | solution.py:34
  73.4 5.5 %copy-start = (bf16[8,8,128,128]{3,2,1,0:T(8,128)(2,1)S(1)}, bf16[8,8,128,128]{3,2,1,0:T(8,128)(2,1)}, u32[]{:S(2)}) copy-start(bf16[8,8,128,128]{3,2,1,0:T(8,128)(2,1)} %all-gather.3.cloned.1.call-done) | copy-start | bytes 6291460
  73.4 5.5 %copy-start.4 = (bf16[4,8,128,128]{3,2,1,0:T(8,128)(2,1)S(1)}, bf16[4,8,128,128]{3,2,1,0:T(8,128)(2,1)}, u32[]{:S(2)}) copy-start(bf16[4,8,128,128]{3,2,1,0:T(8,128)(2,1)} %all-gather.5.cloned.1.call-done) | copy-start | bytes 3145732
  103.3 6.1 %copy-start.1 = (f32[8,8,128,128]{3,0,2,1:T(8,128)S(1)}, f32[8,8,128,128]{3,0,2,1:T(8,128)}, u32[]{:S(2)}) copy-start(f32[8,8,128,128]{3,0,2,1:T(8,128)} %copy.26) | copy-start | bytes 12582916
  103.3 9.9 %copy-start.2 = (f32[8,8,128,128]{3,0,2,1:T(8,128)S(1)}, f32[8,8,128,128]{3,0,2,1:T(8,128)}, u32[]{:S(2)}) copy-start(f32[8,8,128,128]{3,0,2,1:T(8,128)} %copy.21) | copy-start | bytes 12582916
  109.4 7.5 %copy-start.3 = (f32[8,8,128,128]{3,0,2,1:T(8,128)S(1)}, f32[8,8,128,128]{3,0,2,1:T(8,128)}, u32[]{:S(2)}) copy-start(f32[8,8,128,128]{3,0,2,1:T(8,128)} %copy.16) | copy-start | bytes 12582916
Sparse Core Ops, SparseCore 0:
  9.2 30.6 all-gather.4
  41.8 27.1 all-gather.2
where the time goes:
time: 129 us
  waiting for transfers between devices  56.6 us (44%)
  matrix products  30 us (23%)
  local copies, waits for them, and re-layouts  21.8 us (17%)
  between operations  13.5 us (10%)
  other arithmetic  7.1 us (6%)
    all_gather x1, waiting for transfers between devices, on_device(): later_full = lax.all_gather(masked_late, 'row', axis=0, tiled=True)  29.1 us
    all_gather x1, waiting for transfers between devices, on_device(): earlier_full = lax.all_gather(masked_early, 'col', axis=1, tiled=True)  27.5 us
    transpose x4, local copies, waits for them, and re-layouts, compose_blocks(): jnp.einsum('kab,kjbc->kjac', earlier_full[row_number], later_full, prefer...  21.6 us
    dot_general x4, matrix products, compose_blocks(): jnp.einsum('jk,kjac->jac', counts[row_number], products, precision=lax.Pr...  17.3 us
    dot_general x4, matrix products, compose_blocks(): jnp.einsum('kab,kjbc->kjac', earlier_full[row_number], later_full, prefer...  12.6 us
  transfers between devices with their start and end apart: 2, of which 2 were waited for; matrix products, arithmetic and copies ran while one was open for 3% of the time, Pallas kernels for 0%

commit v1 on v0

v1 whole, which is shorter than its diff:
```python
import functools

import jax
import jax.numpy as jnp
from jax import lax
from jax.experimental import pallas as pl
from jax.experimental.pallas import tpu as pltpu
from jax.sharding import PartitionSpec as P

MESH = pl.DeviceIdType.MESH
LANES = 128


def slot_positions(pattern_ref, capacity):
    count_a, count_b = pattern_ref.shape
    slots = []
    for slot in range(capacity):
        at_a, at_b, found = jnp.int32(0), jnp.int32(0), jnp.int32(0)
        rank = jnp.int32(0)
        for a in range(count_a):
            for b in range(count_b):
                live = pattern_ref[a, b]
                hit = jnp.logical_and(live == 1, rank == slot)
                at_a = jnp.where(hit, a, at_a)
                at_b = jnp.where(hit, b, at_b)
                found = jnp.where(hit, 1, found)
                rank = rank + live
        slots.append((at_a, at_b, found))
    return slots


def pack(blocks_ref, pattern_ref, packed_ref, meta_ref):
    lane = lax.broadcasted_iota(jnp.int32, meta_ref.shape, 1)
    meta = jnp.zeros(meta_ref.shape, jnp.int32)
    for slot, (at_a, at_b, found) in enumerate(slot_positions(pattern_ref, packed_ref.shape[0])):
        packed_ref[slot] = blocks_ref[at_a, at_b]
        for part, value in enumerate((at_a, at_b, found)):
            meta = jnp.where(lane == 3 * slot + part, value, meta)
    meta_ref[...] = meta


def gather_kernel(
    n_row, n_col, middle,
    e_ref, l_ref, ep_ref, lp_ref, t_ref,
    eg_ref, lg_ref, em_ref, lm_ref, cnt_ref,
    pe_ref, pl_ref, me_ref, ml_ref,
    send_e, recv_e, send_l, recv_l, send_f, recv_f, local_sem,
):
    row, col = lax.axis_index("row"), lax.axis_index("col")
    partner = row + 1 - 2 * lax.rem(row, 2)
    row_steps = range(1, n_row // 2)
    col_steps = range(1, n_col)
    row_to = [(lax.rem(row + 2 * d, n_row), col) for d in row_steps]
    col_to = [(row, lax.rem(col + d, n_col)) for d in col_steps]

    barrier = pltpu.get_barrier_semaphore()
    others = row_to + col_to + [(partner, col)]
    for other in others:
        pl.semaphore_signal(barrier, inc=1, device_id=other, device_id_type=MESH)
    pack(l_ref, lp_ref, pl_ref, ml_ref)
    pack(e_ref, ep_ref, pe_ref, me_ref)
    pl.semaphore_wait(barrier, len(others))

    def remote(src, dst, send, recv, device):
        return pltpu.make_async_remote_copy(
            src_ref=src, dst_ref=dst, send_sem=send, recv_sem=recv,
            device_id=device, device_id_type=MESH,
        )

    def pair(srcs, dsts, where, send, recv, d, device):
        return [
            remote(srcs[n], dsts[n].at[where], send.at[n, d], recv.at[n, d], device)
            for n in range(2)
        ]

    later_out, earlier_out = (lg_ref, lm_ref), (eg_ref, em_ref)
    later_own, earlier_own = (pl_ref, ml_ref), (pe_ref, me_ref)
    to_rows = [
        pair(later_own, later_out, row, send_l, recv_l, d, device)
        for d, device in zip(row_steps, row_to)
    ]
    to_cols = [
        pair(earlier_own, earlier_out, col, send_e, recv_e, d, device)
        for d, device in zip(col_steps, col_to)
    ]
    forwards = [pair(later_own, later_out, row, send_f, recv_f, 0, (partner, col))]
    for group in to_rows + to_cols + forwards:
        for copy in group:
            copy.start()
    locals_ = [
        pltpu.make_async_copy(src, dst, local_sem.at[n])
        for n, (src, dst) in enumerate((
            (pl_ref, lg_ref.at[row]), (ml_ref, lm_ref.at[row]),
            (pe_ref, eg_ref.at[col]), (me_ref, em_ref.at[col]),
        ))
    ]
    for copy in locals_:
        copy.start()

    rows, cols, listed = t_ref.shape
    lane = lax.broadcasted_iota(jnp.int32, (cols, LANES), 1)
    for i in range(rows):
        numbers = t_ref[i]
        counts = jnp.zeros((cols, LANES), jnp.float32)
        for k in range(middle):
            hits = jnp.sum(jnp.where(numbers == k, 1.0, 0.0), axis=1, keepdims=True)
            counts = jnp.where(lane == k, hits, counts)
        cnt_ref[pl.ds(i * cols, cols), :] = counts

    for d, group in zip(row_steps, to_rows):
        for copy in group:
            copy.wait_recv()
        source = lax.rem(row + n_row - 2 * d, n_row)
        onward = pair(
            (lg_ref.at[source], lm_ref.at[source]), later_out, source,
            send_f, recv_f, d, (partner, col),
        )
        for copy in onward:
            copy.start()
        forwards.append(onward)
    for group in to_cols + forwards:
        for copy in group:
            copy.wait_recv()
    for group in to_rows + to_cols + forwards:
        for copy in group:
            copy.wait_send()
    for copy in locals_:
        copy.wait()


def compose_kernel(early_ka, late_kb, eg_ref, lg_ref, em_ref, lm_ref, cnt_ref, out_ref):
    n_col, slots_e = eg_ref.shape[:2]
    slots_l = lg_ref.shape[1]
    rows, cols = out_ref.shape[:2]
    out_ref[...] = jnp.zeros_like(out_ref)
    for c in range(n_col):
        for s in range(slots_e):
            i = em_ref[c, 0, 3 * s]
            k = c * early_ka + em_ref[c, 0, 3 * s + 1]
            live_e = em_ref[c, 0, 3 * s + 2]
            source = k // late_kb if late_kb > 1 else k
            later = jnp.concatenate([lg_ref[source, u] for u in range(slots_l)], axis=1)
            product = jnp.dot(eg_ref[c, s], later, preferred_element_type=jnp.float32)
            for u in range(slots_l):
                k_l = source * late_kb + lm_ref[source, 0, 3 * u]
                j = lm_ref[source, 0, 3 * u + 1]
                live = jnp.logical_and(live_e * lm_ref[source, 0, 3 * u + 2] == 1, k_l == k)
                weight = jnp.where(live, cnt_ref[i * cols + j, k], 0.0)
                out_ref[i, j] += weight * product[:, u * LANES:(u + 1) * LANES]


def on_device(n_row, n_col, earlier_blocks, later_blocks, earlier_pattern, later_pattern, triples):
    rows, early_ka, side, _ = earlier_blocks.shape
    late_kb, cols = later_blocks.shape[:2]
    slots_e = max(1, rows * early_ka // 2)
    slots_l = max(1, late_kb * cols // 2)
    middle = n_row * late_kb
    vmem = pl.BlockSpec(memory_space=pltpu.VMEM)
    smem = pl.BlockSpec(memory_space=pltpu.SMEM)
    hbm = pl.BlockSpec(memory_space=pl.ANY)
    block = jnp.bfloat16
    eg, lg, em, lm, counts = pl.pallas_call(
        functools.partial(gather_kernel, n_row, n_col, middle),
        out_shape=(
            jax.ShapeDtypeStruct((n_col, slots_e, side, side), block),
            jax.ShapeDtypeStruct((n_row, slots_l, side, side), block),
            jax.ShapeDtypeStruct((n_col, 1, LANES), jnp.int32),
            jax.ShapeDtypeStruct((n_row, 1, LANES), jnp.int32),
            jax.ShapeDtypeStruct((rows * cols, LANES), jnp.float32),
        ),
        in_specs=[vmem, vmem, smem, smem, vmem],
        out_specs=(hbm, hbm, hbm, hbm, vmem),
        scratch_shapes=[
            pltpu.VMEM((slots_e, side, side), block),
            pltpu.VMEM((slots_l, side, side), block),
            pltpu.VMEM((1, LANES), jnp.int32),
            pltpu.VMEM((1, LANES), jnp.int32),
            pltpu.SemaphoreType.DMA((2, n_col)),
            pltpu.SemaphoreType.DMA((2, n_col)),
            pltpu.SemaphoreType.DMA((2, n_row)),
            pltpu.SemaphoreType.DMA((2, n_row)),
            pltpu.SemaphoreType.DMA((2, n_row)),
            pltpu.SemaphoreType.DMA((2, n_row)),
            pltpu.SemaphoreType.DMA((4,)),
        ],
        compiler_params=pltpu.CompilerParams(collective_id=0, has_side_effects=True),
        name="gather_live",
    )(earlier_blocks, later_blocks, earlier_pattern, later_pattern, triples)
    return pl.pallas_call(
        functools.partial(compose_kernel, early_ka, late_kb),
        out_shape=jax.ShapeDtypeStruct((rows, cols, side, side), jnp.float32),
        in_specs=[vmem, vmem, smem, smem, smem],
        out_specs=vmem,
        name="compose",
    )(eg, lg, em, lm, counts)


def solution(mesh):
    return jax.shard_map(
        functools.partial(on_device, mesh.shape["row"], mesh.shape["col"]),
        mesh=mesh,
        in_specs=(
            P("row", "col", None, None),
            P("row", "col", None, None),
            P("row", "col"),
            P("row", "col"),
            P("row", "col", None),
        ),
        out_specs=P("row", "col", None, None),
        check_vma=False,
    )
```

time: 129 us -> 24.2 us (0.19)
  waiting for transfers between devices: 56.6 us -> 0 us
  matrix products: 30 us -> 0 us
  Pallas kernels: 0 us -> 22.7 us
  local copies, waits for them, and re-layouts: 21.8 us -> 1.34 us
  between operations: 13.5 us -> 0.01 us
  other arithmetic: 7.1 us -> 0 us
    all_gather x2 -> x0, waiting for transfers between devices: 56.6 us -> none  [the longest x1 29.1 us: on_device(): later_full = lax.all_gather(masked_late, 'row', axis=0, tiled=True)]
    dot_general x8 -> x0, matrix products: 30 us -> none  [the longest x4 17.3 us: compose_blocks(): jnp.einsum('jk,kjac->jac', counts[row_number], products, precision=lax.Pr...]
    pallas_call x0 -> x2, Pallas kernels: none -> 22.7 us  [the longest x1 19.1 us: on_device(): pl.pallas_call(functools.partial(gather_kernel, n_row, n_col, middle), ou...]
    transpose x4 -> x0, local copies, waits for them, and re-layouts: 21.6 us -> none  [compose_blocks(): jnp.einsum('kab,kjbc->kjac', earlier_full[row_number], later_full, prefer...]
    mul x2 -> x0, other arithmetic: 3.47 us -> none  [the longest x1 1.74 us: on_device(): later_blocks * later_pattern[:, :, None, None].astype(later_blocks.dtype)]
    another operation x1 -> x0, other arithmetic: 1.46 us -> none  [compose_blocks(): return jnp.stack(results, axis=0)]
    convert_element_type x2 -> x0, other arithmetic: 1.34 us -> none  [the longest x1 0.68 us: on_device(): earlier_pattern[:, :, None, None].astype(earlier_blocks.dtype)]
    unnamed x10 -> x1, local copies, waits for them, and re-layouts: 0.02 us -> 1.34 us
  transfers between devices with their start and end apart: 2 -> 0, of which waited for: 2 -> 0; matrix products, arithmetic and copies ran while one was open for 3% -> 0% of each run, Pallas kernels for 0% -> 0%
where the time goes in v1:
time: 24.2 us; the launch traced here: 24 us
  Pallas kernels  22.7 us (94%)
  local copies, waits for them, and re-layouts  1.34 us (6%)
    pallas_call x1, Pallas kernels, on_device(): pl.pallas_call(functools.partial(gather_kernel, n_row, n_col, middle), ou...  19.1 us
    pallas_call x1, Pallas kernels, on_device(): pl.pallas_call(functools.partial(compose_kernel, early_ka, late_kb), out_...  3.56 us
    unnamed x1, local copies, waits for them, and re-layouts  1.34 us

profile of v1, /device:TPU:0, one launch (start us, length us, event | category | flops | bytes accessed | tf_op | source)
XLA Modules:
  0.0 24.0 jit_solution(14685948464010159879)
XLA Ops:
  0.0 1.3 %copy.6.ep_ref = s32[4,2]{1,0:T(4,128)} copy(s32[4,2]{0,1:T(2,128)} %param.7) | data formatting | bytes 64 | tf_op args[2]
  1.3 19.1 %gather_live.1 = (bf16[4,4,128,128]{3,2,1,0:T(8,128)(2,1)}, bf16[8,4,128,128]{3,2,1,0:T(8,128)(2,1)}, s32[4,1,128]{2,1,0:T(1,128)}, s32[8,1,128]{2,1,0:T(1,128)}, f32[32,128]{1,0:T(8,128)}) custom-call(bf16[4,2,128,128]{3,2,1,0:T(8,128)(2,1)} %e_ref.1, bf16[1,8,128,128]{3,2,1,0:T(8,128)(2,1)} %l_ref.1, s32[4,2]{1,0:T(4,128)} %copy.6.ep_ref, s32[1,8]{1,0:T(1,128)} %lp_ref.1, ...), custom_call_target="tpu_custom_call" | custom-call | tf_op jit(solution)/shard_map/gather_live/pallas_call | solution.py:162
  20.5 3.6 %compose.1 = f32[4,8,128,128]{3,2,1,0:T(8,128)} custom-call(bf16[4,4,128,128]{3,2,1,0:T(8,128)(2,1)} %get-tuple-element.10.eg_ref, bf16[8,4,128,128]{3,2,1,0:T(8,128)(2,1)} %get-tuple-element.11.lg_ref, s32[4,1,128]{2,1,0:T(1,128)} %get-tuple-element.12.em_ref, s32[8,1,128]{2,1,0:T(1,128)} %get-tuple-element.13.lm_ref, f32[32,128]{1,0:T(8,128)} %get-tuple-element.14.cnt_ref), custom_call_target="tpu_custom_call" | custom-call | tf_op jit(solution)/shard_map/compose/pallas_call | solution.py:189

commit v2 on v1

--- a/solution.py
+++ b/solution.py
@@ -11,15 +11,14 @@
 LANES = 128
 
 
-def slot_positions(pattern_ref, capacity):
-    count_a, count_b = pattern_ref.shape
+def slot_positions(pattern, count_a, count_b, capacity):
     slots = []
     for slot in range(capacity):
         at_a, at_b, found = jnp.int32(0), jnp.int32(0), jnp.int32(0)
         rank = jnp.int32(0)
         for a in range(count_a):
             for b in range(count_b):
-                live = pattern_ref[a, b]
+                live = pattern(a, b)
                 hit = jnp.logical_and(live == 1, rank == slot)
                 at_a = jnp.where(hit, a, at_a)
                 at_b = jnp.where(hit, b, at_b)
@@ -29,10 +28,11 @@
     return slots
 
 
-def pack(blocks_ref, pattern_ref, packed_ref, meta_ref):
+def pack(blocks_ref, pattern, packed_ref, meta_ref):
     lane = lax.broadcasted_iota(jnp.int32, meta_ref.shape, 1)
     meta = jnp.zeros(meta_ref.shape, jnp.int32)
-    for slot, (at_a, at_b, found) in enumerate(slot_positions(pattern_ref, packed_ref.shape[0])):
+    slots = slot_positions(pattern, *blocks_ref.shape[:2], packed_ref.shape[0])
+    for slot, (at_a, at_b, found) in enumerate(slots):
         packed_ref[slot] = blocks_ref[at_a, at_b]
         for part, value in enumerate((at_a, at_b, found)):
             meta = jnp.where(lane == 3 * slot + part, value, meta)
@@ -49,17 +49,25 @@
     row, col = lax.axis_index("row"), lax.axis_index("col")
     partner = row + 1 - 2 * lax.rem(row, 2)
     row_steps = range(1, n_row // 2)
-    col_steps = range(1, n_col)
     row_to = [(lax.rem(row + 2 * d, n_row), col) for d in row_steps]
-    col_to = [(row, lax.rem(col + d, n_col)) for d in col_steps]
+    slots_e = pe_ref.shape[0]
+    has_right = col < n_col - 1
+    has_left = col > 0
 
     barrier = pltpu.get_barrier_semaphore()
-    others = row_to + col_to + [(partner, col)]
+    others = row_to + [(partner, col)]
     for other in others:
         pl.semaphore_signal(barrier, inc=1, device_id=other, device_id_type=MESH)
-    pack(l_ref, lp_ref, pl_ref, ml_ref)
-    pack(e_ref, ep_ref, pe_ref, me_ref)
-    pl.semaphore_wait(barrier, len(others))
+    for there, step in ((has_right, 1), (has_left, -1)):
+        @pl.when(there)
+        def _():
+            pl.semaphore_signal(
+                barrier, inc=1, device_id=(row, col + step), device_id_type=MESH
+            )
+    pack(e_ref, lambda a, b: ep_ref[b, a], pe_ref, me_ref)
+    pack(l_ref, lambda a, b: lp_ref[a, b], pl_ref, ml_ref)
+    ends = has_right.astype(jnp.int32) + has_left.astype(jnp.int32)
+    pl.semaphore_wait(barrier, len(others) + ends)
 
     def remote(src, dst, send, recv, device):
         return pltpu.make_async_remote_copy(
@@ -73,18 +81,43 @@
             for n in range(2)
         ]
 
-    later_out, earlier_out = (lg_ref, lm_ref), (eg_ref, em_ref)
-    later_own, earlier_own = (pl_ref, ml_ref), (pe_ref, me_ref)
+    def along(way, hop, chunk):
+        step = 1 - 2 * way
+        source = col - step * hop
+        if chunk == slots_e:
+            src = me_ref if hop == 0 else em_ref.at[source]
+            dst = em_ref.at[source]
+        else:
+            src = pe_ref.at[chunk] if hop == 0 else eg_ref.at[source, chunk]
+            dst = eg_ref.at[source, chunk]
+        return remote(
+            src, dst, send_e.at[way, hop, chunk], recv_e.at[way, hop, chunk],
+            (row, col + step),
+        )
+
+    def sends(way, hop):
+        if way == 0:
+            return jnp.logical_and(has_right, col >= hop)
+        return jnp.logical_and(has_left, col + hop < n_col)
+
+    def receives(way, hop):
+        return col >= hop + 1 if way == 0 else col + hop + 1 < n_col
+
+    hops = range(n_col - 1)
+    chunks = range(slots_e + 1)
+    for chunk in chunks:
+        for way in range(2):
+            @pl.when(sends(way, 0))
+            def _():
+                along(way, 0, chunk).start()
+
+    later_out, later_own = (lg_ref, lm_ref), (pl_ref, ml_ref)
     to_rows = [
         pair(later_own, later_out, row, send_l, recv_l, d, device)
         for d, device in zip(row_steps, row_to)
     ]
-    to_cols = [
-        pair(earlier_own, earlier_out, col, send_e, recv_e, d, device)
-        for d, device in zip(col_steps, col_to)
-    ]
     forwards = [pair(later_own, later_out, row, send_f, recv_f, 0, (partner, col))]
-    for group in to_rows + to_cols + forwards:
+    for group in to_rows + forwards:
         for copy in group:
             copy.start()
     locals_ = [
@@ -107,6 +140,19 @@
             counts = jnp.where(lane == k, hits, counts)
         cnt_ref[pl.ds(i * cols, cols), :] = counts
 
+    def land(hop):
+        for chunk in chunks:
+            for way in range(2):
+                @pl.when(receives(way, hop))
+                def _():
+                    along(way, hop, chunk).wait_recv()
+                if hop + 1 < n_col - 1:
+                    @pl.when(sends(way, hop + 1))
+                    def _():
+                        along(way, hop + 1, chunk).start()
+
+    for hop in hops[:-1]:
+        land(hop)
     for d, group in zip(row_steps, to_rows):
         for copy in group:
             copy.wait_recv()
@@ -118,12 +164,20 @@
         for copy in onward:
             copy.start()
         forwards.append(onward)
-    for group in to_cols + forwards:
+    for hop in hops[-1:]:
+        land(hop)
+    for group in forwards:
         for copy in group:
             copy.wait_recv()
-    for group in to_rows + to_cols + forwards:
+    for group in to_rows + forwards:
         for copy in group:
             copy.wait_send()
+    for hop in hops:
+        for way in range(2):
+            @pl.when(sends(way, hop))
+            def _():
+                for chunk in chunks:
+                    along(way, hop, chunk).wait_send()
     for copy in locals_:
         copy.wait()
 
@@ -175,8 +229,8 @@
             pltpu.VMEM((slots_l, side, side), block),
             pltpu.VMEM((1, LANES), jnp.int32),
             pltpu.VMEM((1, LANES), jnp.int32),
-            pltpu.SemaphoreType.DMA((2, n_col)),
-            pltpu.SemaphoreType.DMA((2, n_col)),
+            pltpu.SemaphoreType.DMA((2, n_col, slots_e + 1)),
+            pltpu.SemaphoreType.DMA((2, n_col, slots_e + 1)),
             pltpu.SemaphoreType.DMA((2, n_row)),
             pltpu.SemaphoreType.DMA((2, n_row)),
             pltpu.SemaphoreType.DMA((2, n_row)),
@@ -185,7 +239,7 @@
         ],
         compiler_params=pltpu.CompilerParams(collective_id=0, has_side_effects=True),
         name="gather_live",
-    )(earlier_blocks, later_blocks, earlier_pattern, later_pattern, triples)
+    )(earlier_blocks, later_blocks, earlier_pattern.T, later_pattern, triples)
     return pl.pallas_call(
         functools.partial(compose_kernel, early_ka, late_kb),
         out_shape=jax.ShapeDtypeStruct((rows, cols, side, side), jnp.float32),

time: 24.2 us -> 23.2 us (0.959)
  local copies, waits for them, and re-layouts: 1.34 us -> 0 us
  Pallas kernels: 22.7 us -> 23 us
    unnamed x1 -> x0, local copies, waits for them, and re-layouts: 1.34 us -> none
    pallas_call x1, Pallas kernels: 19.1 us -> 19.4 us  [on_device(): pl.pallas_call(functools.partial(gather_kernel, n_row, n_col, middle), ou...]
where the time goes in v2:
time: 23.2 us; the launch traced here: 23 us
  Pallas kernels  23 us (99%)
    pallas_call x1, Pallas kernels, on_device(): pl.pallas_call(functools.partial(gather_kernel, n_row, n_col, middle), ou...  19.4 us
    pallas_call x1, Pallas kernels, on_device(): pl.pallas_call(functools.partial(compose_kernel, early_ka, late_kb), out_...  3.55 us

profile of v2, /device:TPU:0, one launch (start us, length us, event | category | flops | bytes accessed | tf_op | source)
XLA Modules:
  0.0 23.0 jit_solution(7134894938087531929)
XLA Ops:
  0.0 19.4 %gather_live.1 = (bf16[4,4,128,128]{3,2,1,0:T(8,128)(2,1)}, bf16[8,4,128,128]{3,2,1,0:T(8,128)(2,1)}, s32[4,1,128]{2,1,0:T(1,128)}, s32[8,1,128]{2,1,0:T(1,128)}, f32[32,128]{1,0:T(8,128)}) custom-call(bf16[4,2,128,128]{3,2,1,0:T(8,128)(2,1)} %e_ref.1, bf16[1,8,128,128]{3,2,1,0:T(8,128)(2,1)} %l_ref.1, s32[2,4]{1,0:T(2,128)} %bitcast.1, s32[1,8]{1,0:T(1,128)} %lp_ref.1, ...), custom_call_target="tpu_custom_call" | custom-call | tf_op jit(solution)/shard_map/gather_live/pallas_call | solution.py:216
  19.4 3.5 %compose.1 = f32[4,8,128,128]{3,2,1,0:T(8,128)} custom-call(bf16[4,4,128,128]{3,2,1,0:T(8,128)(2,1)} %get-tuple-element.10.eg_ref, bf16[8,4,128,128]{3,2,1,0:T(8,128)(2,1)} %get-tuple-element.11.lg_ref, s32[4,1,128]{2,1,0:T(1,128)} %get-tuple-element.12.em_ref, s32[8,1,128]{2,1,0:T(1,128)} %get-tuple-element.13.lm_ref, f32[32,128]{1,0:T(8,128)} %get-tuple-element.14.cnt_ref), custom_call_target="tpu_custom_call" | custom-call | tf_op jit(solution)/shard_map/compose/pallas_call | solution.py:243

commit v3 on v2

--- a/solution.py
+++ b/solution.py
@@ -41,10 +41,10 @@
 
 def gather_kernel(
     n_row, n_col, middle,
-    e_ref, l_ref, ep_ref, lp_ref, t_ref,
+    e_hbm, l_hbm, ep_ref, lp_ref, t_ref,
     eg_ref, lg_ref, em_ref, lm_ref, cnt_ref,
-    pe_ref, pl_ref, me_ref, ml_ref,
-    send_e, recv_e, send_l, recv_l, send_f, recv_f, local_sem,
+    e_ref, l_ref, pe_ref, pl_ref, me_ref, ml_ref,
+    send_e, recv_e, send_l, recv_l, send_f, recv_f, local_sem, fetch_sem,
 ):
     row, col = lax.axis_index("row"), lax.axis_index("col")
     partner = row + 1 - 2 * lax.rem(row, 2)
@@ -64,7 +64,13 @@
             pl.semaphore_signal(
                 barrier, inc=1, device_id=(row, col + step), device_id_type=MESH
             )
+    fetch_e = pltpu.make_async_copy(e_hbm, e_ref, fetch_sem.at[0])
+    fetch_l = pltpu.make_async_copy(l_hbm, l_ref, fetch_sem.at[1])
+    fetch_e.start()
+    fetch_l.start()
+    fetch_e.wait()
     pack(e_ref, lambda a, b: ep_ref[b, a], pe_ref, me_ref)
+    fetch_l.wait()
     pack(l_ref, lambda a, b: lp_ref[a, b], pl_ref, ml_ref)
     ends = has_right.astype(jnp.int32) + has_left.astype(jnp.int32)
     pl.semaphore_wait(barrier, len(others) + ends)
@@ -182,11 +188,22 @@
         copy.wait()
 
 
-def compose_kernel(early_ka, late_kb, eg_ref, lg_ref, em_ref, lm_ref, cnt_ref, out_ref):
+def compose_kernel(
+    early_ka, late_kb,
+    eg_hbm, lg_hbm, em_ref, lm_ref, cnt_ref, out_ref, eg_ref, lg_ref, fetch_sem,
+):
+    fetches = [
+        pltpu.make_async_copy(lg_hbm, lg_ref, fetch_sem.at[0]),
+        pltpu.make_async_copy(eg_hbm, eg_ref, fetch_sem.at[1]),
+    ]
+    for copy in fetches:
+        copy.start()
     n_col, slots_e = eg_ref.shape[:2]
     slots_l = lg_ref.shape[1]
     rows, cols = out_ref.shape[:2]
     out_ref[...] = jnp.zeros_like(out_ref)
+    for copy in fetches:
+        copy.wait()
     for c in range(n_col):
         for s in range(slots_e):
             i = em_ref[c, 0, 3 * s]
@@ -222,9 +239,11 @@
             jax.ShapeDtypeStruct((n_row, 1, LANES), jnp.int32),
             jax.ShapeDtypeStruct((rows * cols, LANES), jnp.float32),
         ),
-        in_specs=[vmem, vmem, smem, smem, vmem],
+        in_specs=[hbm, hbm, smem, smem, vmem],
         out_specs=(hbm, hbm, hbm, hbm, vmem),
         scratch_shapes=[
+            pltpu.VMEM(earlier_blocks.shape, block),
+            pltpu.VMEM(later_blocks.shape, block),
             pltpu.VMEM((slots_e, side, side), block),
             pltpu.VMEM((slots_l, side, side), block),
             pltpu.VMEM((1, LANES), jnp.int32),
@@ -236,6 +255,7 @@
             pltpu.SemaphoreType.DMA((2, n_row)),
             pltpu.SemaphoreType.DMA((2, n_row)),
             pltpu.SemaphoreType.DMA((4,)),
+            pltpu.SemaphoreType.DMA((2,)),
         ],
         compiler_params=pltpu.CompilerParams(collective_id=0, has_side_effects=True),
         name="gather_live",
@@ -243,8 +263,13 @@
     return pl.pallas_call(
         functools.partial(compose_kernel, early_ka, late_kb),
         out_shape=jax.ShapeDtypeStruct((rows, cols, side, side), jnp.float32),
-        in_specs=[vmem, vmem, smem, smem, smem],
+        in_specs=[hbm, hbm, smem, smem, smem],
         out_specs=vmem,
+        scratch_shapes=[
+            pltpu.VMEM(eg.shape, block),
+            pltpu.VMEM(lg.shape, block),
+            pltpu.SemaphoreType.DMA((2,)),
+        ],
         name="compose",
     )(eg, lg, em, lm, counts)
 

time: 23.2 us -> 24 us (1.034)
  Pallas kernels: 23 us -> 23.6 us
    pallas_call x1, Pallas kernels: 3.55 us -> 4.5 us  [on_device(): pl.pallas_call(functools.partial(compose_kernel, early_ka, late_kb), out_...]
    pallas_call x1, Pallas kernels: 19.4 us -> 19.1 us  [on_device(): pl.pallas_call(functools.partial(gather_kernel, n_row, n_col, middle), ou...]
where the time goes in v3:
time: 24 us; the launch traced here: 23.7 us
  Pallas kernels  23.6 us (98%)
    pallas_call x1, Pallas kernels, on_device(): pl.pallas_call(functools.partial(gather_kernel, n_row, n_col, middle), ou...  19.1 us
    pallas_call x1, Pallas kernels, on_device(): pl.pallas_call(functools.partial(compose_kernel, early_ka, late_kb), out_...  4.5 us

profile of v3, /device:TPU:0, one launch (start us, length us, event | category | flops | bytes accessed | tf_op | source)
XLA Modules:
  0.0 23.7 jit_solution(1384891471058786839)
XLA Ops:
  0.0 19.1 %gather_live.1 = (bf16[4,4,128,128]{3,2,1,0:T(8,128)(2,1)}, bf16[8,4,128,128]{3,2,1,0:T(8,128)(2,1)}, s32[4,1,128]{2,1,0:T(1,128)}, s32[8,1,128]{2,1,0:T(1,128)}, f32[32,128]{1,0:T(8,128)}) custom-call(bf16[4,2,128,128]{3,2,1,0:T(8,128)(2,1)} %e_hbm.1, bf16[1,8,128,128]{3,2,1,0:T(8,128)(2,1)} %l_hbm.1, s32[2,4]{1,0:T(2,128)} %bitcast.1, s32[1,8]{1,0:T(1,128)} %lp_ref.1, ...), custom_call_target="tpu_custom_call" | custom-call | tf_op jit(solution)/shard_map/gather_live/pallas_call | solution.py:233
  19.1 4.5 %compose.1 = f32[4,8,128,128]{3,2,1,0:T(8,128)} custom-call(bf16[4,4,128,128]{3,2,1,0:T(8,128)(2,1)} %get-tuple-element.10.eg_hbm, bf16[8,4,128,128]{3,2,1,0:T(8,128)(2,1)} %get-tuple-element.11.lg_hbm, s32[4,1,128]{2,1,0:T(1,128)} %get-tuple-element.12.em_ref, s32[8,1,128]{2,1,0:T(1,128)} %get-tuple-element.13.lm_ref, f32[32,128]{1,0:T(8,128)} %get-tuple-element.14.cnt_ref), custom_call_target="tpu_custom_call" | custom-call | tf_op jit(solution)/shard_map/compose/pallas_call | solution.py:263

commit v4 on v2

--- a/solution.py
+++ b/solution.py
@@ -41,10 +41,10 @@
 
 def gather_kernel(
     n_row, n_col, middle,
-    e_ref, l_ref, ep_ref, lp_ref, t_ref,
+    e_hbm, l_hbm, ep_ref, lp_ref, t_ref,
     eg_ref, lg_ref, em_ref, lm_ref, cnt_ref,
-    pe_ref, pl_ref, me_ref, ml_ref,
-    send_e, recv_e, send_l, recv_l, send_f, recv_f, local_sem,
+    e_ref, l_ref, pe_ref, pl_ref, me_ref, ml_ref,
+    send_e, recv_e, send_l, recv_l, send_f, recv_f, local_sem, fetch_sem,
 ):
     row, col = lax.axis_index("row"), lax.axis_index("col")
     partner = row + 1 - 2 * lax.rem(row, 2)
@@ -64,7 +64,13 @@
             pl.semaphore_signal(
                 barrier, inc=1, device_id=(row, col + step), device_id_type=MESH
             )
+    fetch_e = pltpu.make_async_copy(e_hbm, e_ref, fetch_sem.at[0])
+    fetch_l = pltpu.make_async_copy(l_hbm, l_ref, fetch_sem.at[1])
+    fetch_e.start()
+    fetch_l.start()
+    fetch_e.wait()
     pack(e_ref, lambda a, b: ep_ref[b, a], pe_ref, me_ref)
+    fetch_l.wait()
     pack(l_ref, lambda a, b: lp_ref[a, b], pl_ref, ml_ref)
     ends = has_right.astype(jnp.int32) + has_left.astype(jnp.int32)
     pl.semaphore_wait(barrier, len(others) + ends)
@@ -222,9 +228,11 @@
             jax.ShapeDtypeStruct((n_row, 1, LANES), jnp.int32),
             jax.ShapeDtypeStruct((rows * cols, LANES), jnp.float32),
         ),
-        in_specs=[vmem, vmem, smem, smem, vmem],
+        in_specs=[hbm, hbm, smem, smem, vmem],
         out_specs=(hbm, hbm, hbm, hbm, vmem),
         scratch_shapes=[
+            pltpu.VMEM(earlier_blocks.shape, block),
+            pltpu.VMEM(later_blocks.shape, block),
             pltpu.VMEM((slots_e, side, side), block),
             pltpu.VMEM((slots_l, side, side), block),
             pltpu.VMEM((1, LANES), jnp.int32),
@@ -236,6 +244,7 @@
             pltpu.SemaphoreType.DMA((2, n_row)),
             pltpu.SemaphoreType.DMA((2, n_row)),
             pltpu.SemaphoreType.DMA((4,)),
+            pltpu.SemaphoreType.DMA((2,)),
         ],
         compiler_params=pltpu.CompilerParams(collective_id=0, has_side_effects=True),
         name="gather_live",

time: 23.2 us -> 23 us (level)
  Pallas kernels: 23 us -> 22.7 us
    pallas_call x1, Pallas kernels: 19.4 us -> 19.1 us  [on_device(): pl.pallas_call(functools.partial(gather_kernel, n_row, n_col, middle), ou...]
where the time goes in v4:
time: 23 us; the launch traced here: 22.7 us
  Pallas kernels  22.7 us (99%)
    pallas_call x1, Pallas kernels, on_device(): pl.pallas_call(functools.partial(gather_kernel, n_row, n_col, middle), ou...  19.1 us
    pallas_call x1, Pallas kernels, on_device(): pl.pallas_call(functools.partial(compose_kernel, early_ka, late_kb), out_...  3.56 us

profile of v4, /device:TPU:0, one launch (start us, length us, event | category | flops | bytes accessed | tf_op | source)
XLA Modules:
  0.0 22.7 jit_solution(1162338825584289277)
XLA Ops:
  0.0 19.1 %gather_live.1 = (bf16[4,4,128,128]{3,2,1,0:T(8,128)(2,1)}, bf16[8,4,128,128]{3,2,1,0:T(8,128)(2,1)}, s32[4,1,128]{2,1,0:T(1,128)}, s32[8,1,128]{2,1,0:T(1,128)}, f32[32,128]{1,0:T(8,128)}) custom-call(bf16[4,2,128,128]{3,2,1,0:T(8,128)(2,1)} %e_hbm.1, bf16[1,8,128,128]{3,2,1,0:T(8,128)(2,1)} %l_hbm.1, s32[2,4]{1,0:T(2,128)} %bitcast.1, s32[1,8]{1,0:T(1,128)} %lp_ref.1, ...), custom_call_target="tpu_custom_call" | custom-call | tf_op jit(solution)/shard_map/gather_live/pallas_call | solution.py:222
  19.1 3.6 %compose.1 = f32[4,8,128,128]{3,2,1,0:T(8,128)} custom-call(bf16[4,4,128,128]{3,2,1,0:T(8,128)(2,1)} %get-tuple-element.10.eg_ref, bf16[8,4,128,128]{3,2,1,0:T(8,128)(2,1)} %get-tuple-element.11.lg_ref, s32[4,1,128]{2,1,0:T(1,128)} %get-tuple-element.12.em_ref, s32[8,1,128]{2,1,0:T(1,128)} %get-tuple-element.13.lm_ref, f32[32,128]{1,0:T(8,128)} %get-tuple-element.14.cnt_ref), custom_call_target="tpu_custom_call" | custom-call | tf_op jit(solution)/shard_map/compose/pallas_call | solution.py:252
